TPU v7x, 256 devices: a whole 4x4x8 slice. The times are simulated.
256 devices in a mesh: gx: 8 (over x, core), gy: 32 (over y, z).
Axes of the slice: x: 4, y: 4, z: 8, core: 2. Of those that a mesh axis runs over, the one named last changes fastest.
Arguments:
- reference_image: bfloat16 [32, 256, 4096], P(None, 'gx', 'gy'), may hold values from -6 to 6
- moving_image: float32 [44, 256, 4096], P(None, 'gx', 'gy'), may hold values from -6 to 6
- image_gradient: bfloat16 [3, 32, 256, 4096], P(None, None, 'gx', 'gy'), may hold values from -1.5 to 1.5
- voxel_shift: int32 [3, 4, 32, 512], P(None, None, 'gx', 'gy'), may hold values from -6 to 5
- subvoxel: float32 [3, 4, 32, 512], P(None, None, 'gx', 'gy'), may hold values from 0 to 1
Outputs:
- increment: float32 [3, 5, 32, 512], P(None, None, 'gx', 'gy')
- cg_residual: float32 [3, 5, 32, 512], P(None, None, 'gx', 'gy')
All inputs are finite; a program needn't handle non-finite values.
Results may differ from a plain program's by a relative error of at most 0.0003.
Values sent between devices are 32-bit elements; how exact they have to be, the bound alone decides.
No kernel may reach another device: no remote copies, remote signals or barrier semaphores. Data moves between devices by JAX's collectives and lax.ppermute only.
A program may use at most 128 MiB of HBM per device.

v0:
```python
import functools

import jax
import jax.numpy as jnp
import numpy as np
from jax import lax
from jax.sharding import Mesh
from jax.sharding import PartitionSpec as P

ELEM = 8
HW = 6
ITERS = 3
GX_GY = ("gx_0", "gx_1", "gy_0", "gy_1")
GX = ("gx_0", "gx_1")
GY = ("gy_0", "gy_1")


ridge_weight = 2.0


def padded_2(cells, sides, width):
    for axis, dim in sides:
        count = lax.axis_size(axis)
        ends = count - 1
        head = lax.slice_in_dim(cells, 0, width, axis=dim)
        tail = lax.slice_in_dim(cells, cells.shape[dim] - width, cells.shape[dim], axis=dim)
        cells = jnp.concatenate(
            [
                lax.ppermute(tail, axis, [(i, (i + 1) % count) for i in range(ends)]),
                cells,
                lax.ppermute(head, axis, [((i + 1) % count, i) for i in range(ends)]),
            ],
            axis=dim,
        )
    return cells


def one_axis_at_a_time(x, axes):
    return functools.reduce(lax.psum, axes, x)


def linear_basis():
    centres = (jnp.arange(ELEM, dtype=jnp.float32) + 0.5) / ELEM
    return jnp.stack([1.0 - centres, centres])


def corner_weights():
    shape_basis = linear_basis()
    return jnp.einsum("pi,qj,rl->pqrijl", shape_basis, shape_basis, shape_basis).reshape(
        8, ELEM * ELEM * ELEM
    )


def corner_sides():
    return [(side_z, side_x, side_y) for side_z in (0, 1) for side_x in (0, 1) for side_y in (0, 1)]


def element_major(volume, count_z, count_x, count_y):
    shaped = volume.reshape(count_z, ELEM, count_x, ELEM, count_y, ELEM)
    return shaped.transpose(1, 3, 5, 0, 2, 4).reshape(
        ELEM * ELEM * ELEM, count_z * count_x * count_y
    )


def element_stiffness(gradient_cols):
    weights = corner_weights()
    pair_weights = (weights[:, None, :] * weights[None, :, :]).reshape(64, ELEM * ELEM * ELEM)
    blocks = {}
    for first_comp in range(3):
        for second_comp in range(first_comp, 3):
            product = gradient_cols[first_comp] * gradient_cols[second_comp]
            summed = jnp.dot(pair_weights, product, precision=lax.Precision.HIGHEST)
            blocks[first_comp, second_comp] = summed.reshape(8, 8, -1)
            blocks[second_comp, first_comp] = blocks[first_comp, second_comp]
    stiff_rows = []
    for first_comp in range(3):
        stiff_rows.append(
            jnp.stack([blocks[first_comp, second_comp] for second_comp in range(3)], axis=2)
        )
    return jnp.stack(stiff_rows, axis=1)


def element_load(image_cols, gradient_cols, warped):
    weights = corner_weights()
    mismatch = image_cols - warped
    load_terms = [
        jnp.dot(weights, gradient_cols[component] * mismatch, precision=lax.Precision.HIGHEST)
        for component in range(3)
    ]
    return jnp.stack(load_terms, axis=1)


def warp_columns(source, start_z, start_x, start_y, weight_z, weight_x, weight_y):

    def cut_block(corner_z, corner_x, corner_y):
        return lax.dynamic_slice(
            source, (corner_z, corner_x, corner_y), (ELEM + 1, ELEM + 1, ELEM + 1)
        )

    gathered = jax.vmap(cut_block, out_axes=3)(start_z, start_x, start_y)
    along_z = (1.0 - weight_z) * gathered[:ELEM] + weight_z * gathered[1:]
    along_x = (1.0 - weight_x) * along_z[:, :ELEM] + weight_x * along_z[:, 1:]
    along_y = (1.0 - weight_y) * along_x[:, :, :ELEM] + weight_y * along_x[:, :, 1:]
    return along_y.reshape(ELEM * ELEM * ELEM, -1)


def nodes_to_elements(nodal_field, count_z, count_x, count_y):
    picked = [
        nodal_field[
            :, side_z : side_z + count_z, side_x : side_x + count_x, side_y : side_y + count_y
        ]
        for side_z, side_x, side_y in corner_sides()
    ]
    return jnp.stack(picked).reshape(8, 3, -1)


def elements_to_nodes(element_terms, count_z, count_x, count_y):
    shaped = element_terms.reshape(8, 3, count_z, count_x, count_y)
    nodal_sum = jnp.zeros((3, count_z + 1, count_x + 1, count_y + 1), jnp.float32)
    for corner_index, (side_z, side_x, side_y) in enumerate(corner_sides()):
        nodal_sum = nodal_sum + jnp.pad(
            shaped[corner_index],
            ((0, 0), (side_z, 1 - side_z), (side_x, 1 - side_x), (side_y, 1 - side_y)),
        )
    return nodal_sum


def element_product(stiffness, element_values):
    return jnp.sum(stiffness * element_values[None, None], axis=(2, 3))


def fold_rims(extended, fold_dim):
    size_along = extended.shape[fold_dim]
    lower_rim = lax.slice_in_dim(extended, 0, 1, axis=fold_dim)
    upper_rim = lax.slice_in_dim(extended, size_along - 1, size_along, axis=fold_dim)
    core_rows = lax.slice_in_dim(extended, 1, size_along - 1, axis=fold_dim)
    first_row = lax.slice_in_dim(core_rows, 0, 1, axis=fold_dim) + lower_rim
    last_row = (
        lax.slice_in_dim(core_rows, size_along - 3, size_along - 2, axis=fold_dim) + upper_rim
    )
    middle = lax.slice_in_dim(core_rows, 1, size_along - 3, axis=fold_dim)
    return jnp.concatenate([first_row, middle, last_row], axis=fold_dim)


def face_sum(nodal_field):
    extended = padded_2(nodal_field, ((GX, 2), (GY, 3)), 1)
    return fold_rims(fold_rims(extended, 2), 3)


def squares(owner_weight, residual):
    return one_axis_at_a_time(jnp.sum(residual * residual * owner_weight), GX_GY)


def is_inner(column, count_x, count_y):
    along_x = column // count_y % count_x
    along_y = column % count_y
    return 1 <= along_x <= count_x - 2 and 1 <= along_y <= count_y - 2


def body(reference_image, moving_image, image_gradient, voxel_shift, subvoxel):
    count_z = voxel_shift.shape[1]
    count_x = voxel_shift.shape[2]
    count_y = voxel_shift.shape[3]
    plane = count_x * count_y
    padded = padded_2(moving_image, ((GX, 1), (GY, 2)), HW)
    gradient_cols = [
        element_major(image_gradient[component], count_z, count_x, count_y).astype(jnp.float32)
        for component in range(3)
    ]
    image_cols = element_major(reference_image, count_z, count_x, count_y).astype(jnp.float32)
    stiffness = element_stiffness(gradient_cols)
    flat_index = jnp.arange(count_z * plane, dtype=jnp.int32)
    elem_z = flat_index // plane
    elem_x = flat_index // count_y % count_x
    elem_y = flat_index % count_y
    start_z = elem_z * ELEM + voxel_shift[0].reshape(-1) + HW
    start_x = elem_x * ELEM + voxel_shift[1].reshape(-1) + HW
    start_y = elem_y * ELEM + voxel_shift[2].reshape(-1) + HW
    weight_z = subvoxel[0].reshape(-1)
    weight_x = subvoxel[1].reshape(-1)
    weight_y = subvoxel[2].reshape(-1)
    total_cols = count_z * plane
    inner_list = [column for column in range(total_cols) if is_inner(column, count_x, count_y)]
    outer_list = [column for column in range(total_cols) if not is_inner(column, count_x, count_y)]
    inner_cols = np.array(inner_list, dtype=np.int32)
    outer_cols = np.array(outer_list, dtype=np.int32)
    local_pad = jnp.pad(moving_image, ((0, 0), (HW, HW), (HW, HW)))
    inner_part = warp_columns(
        local_pad,
        start_z[inner_cols],
        start_x[inner_cols],
        start_y[inner_cols],
        weight_z[inner_cols],
        weight_x[inner_cols],
        weight_y[inner_cols],
    )
    outer_part = warp_columns(
        padded,
        start_z[outer_cols],
        start_x[outer_cols],
        start_y[outer_cols],
        weight_z[outer_cols],
        weight_x[outer_cols],
        weight_y[outer_cols],
    )
    warped = jnp.zeros((ELEM * ELEM * ELEM, count_z * plane), jnp.float32)
    warped = warped.at[:, inner_cols].set(inner_part).at[:, outer_cols].set(outer_part)
    load_flat = element_load(image_cols, gradient_cols, warped)
    load_nodes = face_sum(elements_to_nodes(load_flat, count_z, count_x, count_y))
    last_x = (lax.axis_index(GX) == lax.axis_size(GX) - 1).astype(jnp.float32)
    last_y = (lax.axis_index(GY) == lax.axis_size(GY) - 1).astype(jnp.float32)
    row_weight = jnp.concatenate([jnp.ones((count_x,), jnp.float32), last_x[None]])
    col_weight = jnp.concatenate([jnp.ones((count_y,), jnp.float32), last_y[None]])
    owner_weight = row_weight[:, None] * col_weight[None, :]
    solution = jnp.zeros_like(load_nodes)
    residual = load_nodes
    direction = load_nodes
    norm_now = squares(owner_weight, residual)
    for iteration in range(ITERS):
        element_values = nodes_to_elements(direction, count_z, count_x, count_y)
        partial_nodes = elements_to_nodes(
            element_product(stiffness, element_values), count_z, count_x, count_y
        )
        image_dir = face_sum(partial_nodes) + ridge_weight * direction
        step_length = norm_now / one_axis_at_a_time(
            jnp.sum(direction * image_dir * owner_weight), GX_GY
        )
        solution = solution + step_length * direction
        residual = residual - step_length * image_dir
        norm_next = squares(owner_weight, residual)
        direction = residual + norm_next / norm_now * direction
        norm_now = norm_next
    return (solution[:, :, :count_x, :count_y], residual[:, :, :count_x, :count_y])


def solution(mesh):
    torus = Mesh(mesh.devices.reshape(4, 2, 4, 8), ("gx_0", "gx_1", "gy_0", "gy_1"))
    placed = (
        P(None, GX, GY),
        P(None, GX, GY),
        P(None, None, GX, GY),
        P(None, None, GX, GY),
        P(None, None, GX, GY),
    )
    return jax.shard_map(
        body,
        mesh=torus,
        in_specs=placed,
        out_specs=(P(None, None, GX, GY), P(None, None, GX, GY)),
        check_vma=False,
    )
```

profile of v0, /device:TPU:8, one launch (start us, length us, event | category | flops | bytes accessed | tf_op | source)
XLA Modules:
  0.0 1553.6 jit_solution(6058556755068327205)
XLA Ops:
  26.7 6.1 reshape.381
  32.9 7.8 copy.135
  40.7 5.3 reshape.377
  46.0 6.1 reshape.383
  52.1 7.8 copy.149
  59.9 5.3 reshape.379
  65.2 6.1 reshape.384
  71.3 7.8 copy.151
  79.2 5.7 reshape.380
  95.4 462.8 %while.2 = (s32[]{:T(128)}, f32[44,44,140]{2,1,0:T(8,128)}, s32[112,3]{0,1:T(4,128)S(1)}, f32[112,9,9,9]{3,2,1,0:T(8,128)}, s32[]{:T(128)}) while((s32[]{:T(128)}, f32[44,44,140]{2,1,0:T(8,128)}, s32[112,3]{0,1:T(4,128)S(1)}, f32[112,9,9,9]{3,2,1,0:T(8,128)}, s32[]{:T(128)}) %tuple.123), condition=%wide.while_cond, body=%wide.while_body.sunk | while | flops 2 | bytes 149617 | solution.py:96
  96.1 3.5 bitcast_dynamic-update-slice_fusion.4
  129.2 3.5 bitcast_dynamic-update-slice_fusion.4
  149.8 3.5 bitcast_dynamic-update-slice_fusion.4
  170.5 3.5 bitcast_dynamic-update-slice_fusion.4
  178.8 3.5 bitcast_dynamic-update-slice_fusion.4
  203.6 3.5 bitcast_dynamic-update-slice_fusion.4
  220.1 3.5 bitcast_dynamic-update-slice_fusion.4
  236.6 3.5 bitcast_dynamic-update-slice_fusion.4
  253.2 3.5 bitcast_dynamic-update-slice_fusion.4
  265.5 3.5 bitcast_dynamic-update-slice_fusion.4
  302.7 3.5 bitcast_dynamic-update-slice_fusion.4
  327.5 3.5 bitcast_dynamic-update-slice_fusion.4
  331.6 3.5 bitcast_dynamic-update-slice_fusion.4
  344.0 3.5 bitcast_dynamic-update-slice_fusion.4
  352.3 3.5 bitcast_dynamic-update-slice_fusion.4
  360.6 3.5 bitcast_dynamic-update-slice_fusion.4
  377.1 3.5 bitcast_dynamic-update-slice_fusion.4
  385.4 3.5 bitcast_dynamic-update-slice_fusion.4
  401.9 3.5 bitcast_dynamic-update-slice_fusion.4
  418.5 3.5 bitcast_dynamic-update-slice_fusion.4
  430.9 3.5 bitcast_dynamic-update-slice_fusion.4
  455.7 3.5 bitcast_dynamic-update-slice_fusion.4
  480.5 3.5 bitcast_dynamic-update-slice_fusion.4
  558.3 4.8 copy.137
  578.0 4.0 collective-permute-start.2
  581.9 5.7 collective-permute-start.3
  596.2 6.1 reshape.382
  602.3 7.8 copy.136
  610.1 5.3 reshape.378
  615.6 7.3 pad_maximum_fusion
  623.0 628.8 %while.3 = (s32[]{:T(128)}, f32[44,44,140]{1,0,2:T(8,128)}, s32[144,3]{0,1:T(4,128)S(1)}, f32[144,9,9,9]{3,2,1,0:T(8,128)}, s32[]{:T(128)}) while((s32[]{:T(128)}, f32[44,44,140]{1,0,2:T(8,128)}, s32[144,3]{0,1:T(4,128)S(1)}, f32[144,9,9,9]{3,2,1,0:T(8,128)}, s32[]{:T(128)}) %tuple.126), condition=%wide.while_cond.1, body=%wide.while_body.1.sunk | while | flops 2 | bytes 88937 | solution.py:96
  1251.8 8.2 copy.145
  1276.8 6.0 collective-permute-start.7
  1296.7 6.7 collective-permute-start.11
  1306.6 11.7 all-reduce.37
  1321.4 9.3 all-reduce.36
  1330.7 19.3 %all-reduce.35 = (f32[]{:T(128)}, f32[]{:T(128)}) all-reduce(f32[]{:T(128)} %get-tuple-element.82, f32[]{:T(128)} %get-tuple-element.83), channel_id=1, replica_groups=mesh['gx_0'=4,'gx_1'=2,'gy_0'=4,'gy_1'=8] {'gy_1'}, use_global_device_ids=true, to_apply=%region_6.7 | all-reduce | flops 2 | bytes 16 | tf_op jit(solution)/shard_map/psum | solution.py:39
  1352.0 8.9 psum.176
  1364.0 9.4 psum.178
  1373.4 14.8 psum.179
  1397.7 3.9 collective-permute-start.14
  1401.6 4.0 collective-permute-start.15
  1409.3 10.7 psum.180
  1423.0 9.3 psum.182
  1432.3 18.6 %psum.183 = f32[]{:T(128)} all-reduce(f32[]{:T(128)} %psum.182), channel_id=1, replica_groups=mesh['gx_0'=4,'gx_1'=2,'gy_0'=4,'gy_1'=8] {'gy_1'}, use_global_device_ids=true, to_apply=%region_23.24 | all-reduce | flops 1 | bytes 8 | tf_op jit(solution)/shard_map/psum | solution.py:39
  1452.9 8.3 psum.184
  1464.4 8.3 psum.186
  1472.7 14.8 psum.187
  1493.5 4.0 collective-permute-done.17
  1497.6 3.9 collective-permute-start.18
  1501.5 4.0 collective-permute-start.19
  1509.1 10.7 psum.188
  1522.9 10.3 psum.190
  1533.2 17.5 %psum.191 = f32[]{:T(128)} all-reduce(f32[]{:T(128)} %psum.190), channel_id=1, replica_groups=mesh['gx_0'=4,'gx_1'=2,'gy_0'=4,'gy_1'=8] {'gy_1'}, use_global_device_ids=true, to_apply=%region_34.35 | all-reduce | flops 1 | bytes 8 | tf_op jit(solution)/shard_map/psum | solution.py:39
  (1347 shorter events, 1141.7 us)
Async XLA Ops:
  0.6 16.5 %copy-start.11 = (f32[3,4,4,16]{3,2,1,0:T(4,128)S(1)}, f32[3,4,4,16]{3,2,1,0:T(4,128)}, u32[]{:S(2)}) copy-start(f32[3,4,4,16]{3,2,1,0:T(4,128)} %param.25) | copy-start | bytes 9220
  2.4 567.3 %collective-permute-start = (f32[44,6,128]{2,0,1:T(8,128)}, f32[44,6,128]{2,0,1:T(8,128)}, u32[]{:S(2)}, u32[]{:S(2)}) collective-permute-start(f32[44,6,128]{2,0,1:T(8,128)} %copy.157), channel_id=1, source_target_pairs={{0,32},{32,64},{64,96},{96,128},{128,160},{160,192},{192,224},{1,3... | collective-permute-start | bytes 405512 | tf_op jit(solution)/shard_map/ppermute | solution.py:29
  5.4 567.4 %collective-permute-start.1 = (f32[44,6,128]{2,0,1:T(8,128)}, f32[44,6,128]{2,0,1:T(8,128)}, u32[]{:S(2)}, u32[]{:S(2)}) collective-permute-start(f32[44,6,128]{2,0,1:T(8,128)} %copy.158), channel_id=1, source_target_pairs={{32,0},{64,32},{96,64},{128,96},{160,128},{192,160},{224,192},{33,... | collective-permute-start | bytes 405512 | tf_op jit(solution)/shard_map/ppermute | solution.py:31
  14.2 12.3 copy-start.9
  18.9 72.9 %copy-start.12 = (f32[144]{0:T(256)}, f32[144]{0:T(256)S(1)}, u32[]{:S(2)}) copy-start(f32[144]{0:T(256)S(1)} %gather_fusion.8) | copy-start | bytes 1732
  21.8 70.5 %copy-start.14 = (f32[144]{0:T(256)}, f32[144]{0:T(256)S(1)}, u32[]{:S(2)}) copy-start(f32[144]{0:T(256)S(1)} %gather_fusion.7) | copy-start | bytes 1732
  24.8 68.1 %copy-start.16 = (f32[144]{0:T(256)}, f32[144]{0:T(256)S(1)}, u32[]{:S(2)}) copy-start(f32[144]{0:T(256)S(1)} %gather_fusion.6) | copy-start | bytes 1732
  45.9 518.1 %copy-start.1 = (f32[512,256]{1,0:T(8,128)}, f32[512,256]{1,0:T(8,128)S(1)}, u32[]{:S(2)}) copy-start(f32[512,256]{1,0:T(8,128)S(1)} %reshape.377) | copy-start | bytes 1572868
  65.2 23.8 %copy-start.2 = (f32[512,256]{1,0:T(8,128)}, f32[512,256]{1,0:T(8,128)S(1)}, u32[]{:S(2)}) copy-start(f32[512,256]{1,0:T(8,128)S(1)} %reshape.379) | copy-start | bytes 1572868
  84.9 10.5 copy-start.3
  84.9 8.6 copy-start.4
  567.2 8.7 copy-start
  575.9 11.8 copy-start.22
  575.9 11.8 copy-start.23
  575.9 11.8 copy-start.24
  578.0 18.2 %copy-start.10 = (bf16[32,32,128]{2,1,0:T(8,128)(2,1)S(1)}, bf16[32,32,128]{2,1,0:T(8,128)(2,1)}, u32[]{:S(2)}) copy-start(bf16[32,32,128]{2,1,0:T(8,128)(2,1)} %param.21) | copy-start | bytes 786436
  578.0 37.6 %collective-permute-start.2 = (f32[44,44,6]{1,0,2:T(8,128)}, f32[44,44,6]{1,0,2:T(8,128)S(1)}, u32[]{:S(2)}, u32[]{:S(2)}) collective-permute-start(f32[44,44,6]{1,0,2:T(8,128)} %get-tuple-element.100), channel_id=1, source_target_pairs={{0,1},{1,2},{2,3},{3,4},{4,5},{5,6},{6,7},{7,8},{8,9},{9,10},{10,1... | collective-permute-start | bytes 139400 | tf_op jit(solution)/shard_map/ppermute | solution.py:29
  581.9 33.7 %collective-permute-start.3 = (f32[44,44,6]{1,0,2:T(8,128)}, f32[44,44,6]{1,0,2:T(8,128)S(1)}, u32[]{:S(2)}, u32[]{:S(2)}) collective-permute-start(f32[44,44,6]{1,0,2:T(8,128)} %get-tuple-element.101), channel_id=1, source_target_pairs={{1,0},{2,1},{3,2},{4,3},{5,4},{6,5},{7,6},{8,7},{9,8},{10,9},{11,1... | collective-permute-start | bytes 139400 | tf_op jit(solution)/shard_map/ppermute | solution.py:31
  1251.8 8.2 copy-start.13
  1251.8 8.2 copy-start.21
  1259.9 0.6 copy-start.15
  1260.0 0.7 copy-start.20
  1260.0 0.8 copy-start.17
  1260.0 0.8 copy-start.19
  1260.6 2.2 copy-start.18
  1262.9 1.3 copy-start.7
  1262.9 1.8 copy-start.8
  1264.2 1.1 copy-start.6
  1264.7 21.8 %copy-start.5 = (f32[8,1,8,3,256]{4,2,0,3,1:T(8,128)S(1)}, f32[8,1,8,3,256]{4,2,0,3,1:T(8,128)}, u32[]{:S(2)}) copy-start(f32[8,1,8,3,256]{4,2,0,3,1:T(8,128)} %get-tuple-element.117) | copy-start | bytes 589828
  1266.8 4.8 collective-permute-start.4
  1270.2 4.6 collective-permute-start.5
  1274.9 8.2 collective-permute-start.6
  1276.8 7.9 collective-permute-start.7
  1287.6 4.6 collective-permute-start.8
  1290.8 3.9 collective-permute-start.9
  1294.8 8.7 collective-permute-start.10
  1296.7 8.4 collective-permute-start.11
  1391.6 2.6 collective-permute-start.12
  1392.9 4.7 collective-permute-start.13
  1397.7 8.2 collective-permute-start.14
  1401.6 6.1 collective-permute-start.15
  1490.9 2.6 collective-permute-start.16
  1492.2 5.3 collective-permute-start.17
  1497.6 8.2 collective-permute-start.18
  1501.5 6.1 collective-permute-start.19
where the time goes:
time: 1580 us; the launch traced here: 1550 us
  local copies, waits for them, and re-layouts  1230 us (78%)
  blocking collectives  197 us (12%)
  starting transfers between devices  60.2 us (4%)
  other arithmetic  27.2 us (2%)
  waiting for transfers between devices  20.7 us (1%)
    gather x1056, local copies, waits for them, and re-layouts  1090 us
    psum x20, blocking collectives, one_axis_at_a_time(): return functools.reduce(lax.psum, axes, x)  197 us
    convert_element_type x12, local copies, waits for them, and re-layouts, body(): element_major(image_gradient[component], count_z, count_x, count_y)  64.3 us
    ppermute x10, starting transfers between devices, padded_2(): lax.ppermute(head, axis, [((i + 1) % count, i) for i in range(ends)])  33 us
  transfers between devices with their start and end apart: 20, of which 11 were waited for; matrix products, arithmetic and copies ran while one was open for 38% of the time, Pallas kernels for 0%

commit v1 on v0

v1 whole, which is shorter than its diff:
```python
import functools

import jax
import jax.numpy as jnp
import numpy as np
from jax import lax
from jax.experimental import pallas as pl
from jax.experimental.pallas import tpu as pltpu
from jax.sharding import Mesh
from jax.sharding import PartitionSpec as P

ELEM = 8
HW = 6
RIDGE = 2.0
GX = ("gx_0", "gx_1")
GY = ("gy_0", "gy_1")

CZ, CX, CY = 4, 4, 16
ZS = 24
LOW, HIGH = 3, 2
PAIRS = ((0, 0), (0, 1), (0, 2), (1, 1), (1, 2), (2, 2))
ROWS = 96
BF = jnp.bfloat16
F32 = jnp.float32

T = (np.arange(ELEM) + 0.5) / ELEM
PHI = np.stack([1.0 - T, T])
QUAD = np.stack([PHI[0] * PHI[0], PHI[0] * PHI[1], PHI[1] * PHI[1]])


def quad_of(p, q):
    return p + q


def bf(a):
    return jnp.asarray(np.asarray(a, np.float32), BF)


def stiff_y_weights():
    w = np.zeros((CZ * 128, 3 * 128))
    for ez in range(CZ):
        for r in range(3):
            for ey in range(CY):
                w[ez * 128 + ey * 8 : ez * 128 + ey * 8 + 8, r * 128 + ez * ZS + ey + LOW] = QUAD[r]
    return w


def stiff_x_weights():
    w = np.zeros((160, 96))
    for zq in range(3):
        for q in range(3):
            for ex in range(CX):
                cols = slice(zq * 32 + ex * 8, zq * 32 + ex * 8 + 8)
                w[(zq * 3 + q) * 8 + LOW + ex, cols] = QUAD[q]
                if ex >= 1:
                    w[96 + (ex - 1) * 9 + zq * 3 + q, cols] = QUAD[q]
                if ex < 2:
                    w[128 + ex * 9 + zq * 3 + q, cols] = QUAD[q]
    return w


def place_x():
    lo = np.zeros((ROWS, 32))
    hi = np.zeros((ROWS, 32))
    for f in range(9):
        for m in range(3):
            lo[f * 8 + m, m * 9 + f] = 1.0
        hi[f * 8 + 7, f] = 1.0
        hi[72 + f, 9 + f] = 1.0
    return lo, hi


def pack_y():
    w = np.zeros((3 * 384, 256))
    for j in range(3):
        for r in range(3):
            for z in range(CZ):
                for m in range(3):
                    w[j * 384 + r * 128 + z * ZS + LOW + 13 + m, j * 36 + r * 12 + z * 3 + m] = 1.0
                for m in range(2):
                    w[j * 384 + r * 128 + z * ZS + LOW + m, 128 + j * 36 + r * 12 + z * 3 + m] = 1.0
    return w


def place_y():
    w = np.zeros((3, 256, 384))
    for j in range(3):
        for r in range(3):
            for z in range(CZ):
                for m in range(3):
                    w[j, j * 36 + r * 12 + z * 3 + m, r * 128 + z * ZS + m] = 1.0
                for m in range(2):
                    w[j, 128 + j * 36 + r * 12 + z * 3 + m, r * 128 + z * ZS + LOW + CY + m] = 1.0
    return w


def load_y_weights():
    w = np.zeros((2 * CZ * 128, 128))
    for side in range(2):
        for ez in range(CZ):
            base = (side * CZ + ez) * 128
            for ey in range(CY):
                for c in range(2):
                    w[base + ey * 8 : base + ey * 8 + 8, (ez + side) * ZS + LOW + ey + c] += PHI[c]
    return w


def load_x_weights():
    w = np.zeros((8, 32))
    for ex in range(CX):
        for b in range(2):
            w[LOW + ex + b, ex * 8 : ex * 8 + 8] += PHI[b]
    return w


def split3(x):
    h = x.astype(BF)
    r = x - h.astype(F32)
    m = r.astype(BF)
    return h, m, (r - m.astype(F32)).astype(BF)


def dot(a, b):
    return jnp.dot(a, b, preferred_element_type=F32)


def dot_right(x, w):
    h, m, l = split3(x)
    return (dot(l, w) + dot(m, w)) + dot(h, w)


def dot_left(w, x):
    h, m, l = split3(x)
    return (dot(w, l) + dot(w, m)) + dot(w, h)


def stiff_kernel(grad, wy, wx, own, up, low, q_acc):
    def step(ez, carry):
        for xb in range(2):
            acc = [[None] * 3 for _ in PAIRS]
            for i in range(ELEM):
                g = [grad[k, ez * ELEM + i, xb * 16 : xb * 16 + 16, :].astype(F32) for k in range(3)]
                for n, (a, b) in enumerate(PAIRS):
                    prod = g[a] * g[b]
                    for zq in range(3):
                        term = prod * float(QUAD[zq, i])
                        acc[n][zq] = term if i == 0 else acc[n][zq] + term
            for n in range(6):
                for zq in range(3):
                    row = (n * 3 + zq) * 32 + xb * 16
                    q_acc[row : row + 16, pl.ds(pl.multiple_of(ez * 128, 128), 128)] = acc[n][zq]
        return carry

    lax.fori_loop(0, CZ, step, 0)
    for n in range(6):
        d = dot_right(q_acc[n * 96 : n * 96 + 96, :], wy[...])
        o = dot_left(wx[...], d)
        own[n] = o[:96]
        up[n] = o[96:128]
        low[n] = o[128:160]


def extend_kernel(own, from_low, from_up, plo, phi, pack, ext, y_up, y_low):
    for g in range(2):
        packed = None
        for j in range(3):
            n = g * 3 + j
            s = own[n] + dot_left(plo[...], from_low[n]) + dot_left(phi[...], from_up[n])
            ext[n] = s
            part = dot_right(s, pack[j * 384 : j * 384 + 384, :])
            packed = part if packed is None else packed + part
        y_up[g] = packed[:, :128]
        y_low[g] = packed[:, 128:]


def strip_kernel(mov, from_low, from_up, y_up, y_low):
    lane = lax.broadcasted_iota(jnp.int32, (48, 128), 1)
    group = lane >> 3
    for zz in range(3):
        acc_up = jnp.zeros((48, 128), F32)
        acc_low = jnp.zeros((48, 128), F32)
        for g in range(16):
            z = zz * 16 + g
            if z >= mov.shape[0]:
                break
            rows = jnp.concatenate([from_low[z], mov[z], from_up[z]], axis=0)
            sel = group == g
            acc_up = jnp.where(sel, pltpu.roll(rows, (8 * g + 8) % 128, 1) if (8 * g + 8) % 128 else rows, acc_up)
            acc_low = jnp.where(sel, pltpu.roll(rows, 8 * g, 1) if g else rows, acc_low)
        y_up[zz] = acc_up
        y_low[zz] = acc_low


def warp_kernel(shift, frac, mov, x_low, x_up, y_low, y_up, image, grad, wly, wlx, load, vol, zz_acc):
    lane = lax.broadcasted_iota(jnp.int32, (8, 128), 1)
    group = lane >> 3
    lane48 = lax.broadcasted_iota(jnp.int32, (48, 128), 1)

    for z in range(mov.shape[0]):
        rows = jnp.concatenate([x_low[z], mov[z], x_up[z]], axis=0)
        vol[0, z] = rows
        zb, g = z // 16, z % 16
        sl, su = y_low[zb], y_up[zb]
        left = pltpu.roll(sl, 128 - 8 * g, 1) if g else sl
        right = pltpu.roll(su, 120 - 8 * g, 1) if g != 15 else su
        edge = jnp.where(lane48 < 64, pltpu.roll(rows, 8, 1), pltpu.roll(rows, 120, 1))
        edge = jnp.where(lane48 < 8, left, edge)
        vol[1, z] = jnp.where(lane48 >= 120, right, edge)

    n_elem = CZ * CX * CY

    def step(it, carry):
        ez = it // 2
        xp = it % 2
        for h in range(2):
            lo = [None] * ELEM
            hi = [None] * ELEM
            wyv = None
            ex = xp * 2 + h
            for ey in range(CY):
                e = (ez * CX + ex) * CY + ey
                z0 = ez * ELEM + shift[e] + HW
                x0 = ex * ELEM + shift[n_elem + e] + 8
                sy = shift[2 * n_elem + e]
                wz, wx, wy = frac[e], frac[n_elem + e], frac[2 * n_elem + e]
                uz, ux = 1.0 - wz, 1.0 - wx
                if ey == 0:
                    tile, amount = 1, 120 - sy
                elif ey == CY - 1:
                    tile, amount = 1, 136 - sy
                else:
                    tile, amount = 0, 128 - sy
                amount_lo = amount & 127
                amount_hi = (amount - 1) & 127
                sel = group == ey
                wyv = jnp.full((8, 128), wy, F32) if ey == 0 else jnp.where(sel, wy, wyv)
                prev = None
                for i in range(ELEM + 1):
                    a = vol[tile, z0 + i, pl.ds(x0, 8), :]
                    b = vol[tile, z0 + i, pl.ds(x0 + 1, 8), :]
                    c = ux * a + wx * b
                    if i:
                        d = uz * prev + wz * c
                        r_lo = pltpu.roll(d, amount_lo, 1)
                        r_hi = pltpu.roll(d, amount_hi, 1)
                        j = i - 1
                        lo[j] = r_lo if ey == 0 else jnp.where(sel, r_lo, lo[j])
                        hi[j] = r_hi if ey == 0 else jnp.where(sel, r_hi, hi[j])
                    prev = c
            uyv = 1.0 - wyv
            x_rows = pl.ds(pl.multiple_of(xp * 16, 16), 16)
            sums = [[None, None] for _ in range(3)]
            for i in range(ELEM):
                warped = uyv * lo[i] + wyv * hi[i]
                z = ez * ELEM + i
                img = image[z, x_rows, :].astype(F32)[h * 8 : h * 8 + 8]
                miss = img - warped
                for k in range(3):
                    gk = grad[k, z, x_rows, :].astype(F32)[h * 8 : h * 8 + 8]
                    prod = gk * miss
                    for side in range(2):
                        term = prod * float(PHI[side, i])
                        sums[k][side] = term if i == 0 else sums[k][side] + term
            for k in range(3):
                for side in range(2):
                    rows8 = pl.ds(pl.multiple_of(k * 32 + xp * 16 + h * 8, 8), 8)
                    zz_acc[rows8, pl.ds(pl.multiple_of((side * CZ + ez) * 128, 128), 128)] = sums[k][side]
        return carry

    lax.fori_loop(0, CZ * 2, step, 0)
    t = dot_right(zz_acc[...], wly[...])
    for k in range(3):
        load[k] = dot_left(wlx[...], t[k * 32 : k * 32 + 32])


def two_sum(a, b):
    s = a + b
    t = s - a
    return s, (a - (s - t)) + (b - t)


def fast_two_sum(a, b):
    s = a + b
    return s, b - (s - a)


def halves(a):
    c = a * 4097.0
    h = c - (c - a)
    return h, a - h


def two_prod(a, b):
    p = a * b
    ah, al = halves(a)
    bh, bl = halves(b)
    return p, ((ah * bh - p) + ah * bl + al * bh) + al * bl


def df_add(x, y):
    s, e = two_sum(x[0], y[0])
    t, f = two_sum(x[1], y[1])
    s, e = fast_two_sum(s, e + t)
    return fast_two_sum(s, e + f)


def df_neg(x):
    return -x[0], -x[1]


def df_sub(x, y):
    return df_add(x, df_neg(y))


def df_mul(x, y):
    p, e = two_prod(x[0], y[0])
    return fast_two_sum(p, e + (x[0] * y[1] + x[1] * y[0]))


def df_div(x, y):
    q1 = x[0] / y[0]
    p = df_mul(y, (q1, jnp.zeros_like(q1)))
    r = df_sub(x, p)
    q2 = r[0] / y[0]
    return fast_two_sum(q1, q2)


def corner_index(a, b, c):
    return a * 4 + b * 2 + c


def gather_corners(low_rows, high_rows):
    out = {}
    for k in range(3):
        for b, base in enumerate((low_rows[k], high_rows[k])):
            for a in range(2):
                for c in range(2):
                    s = a * ZS + c
                    out[corner_index(a, b, c), k] = pltpu.roll(base, 128 - s, 1) if s else base
    return out


def product(coef, values):
    acc = {}
    for n, (k1, k2) in enumerate(PAIRS):
        for zq in range(3):
            for q in range(3):
                for r in range(3):
                    s = coef(n, zq, q, r)
                    for a in ((0, 0), (0, 1), (1, 0), (1, 1)):
                        if sum(a) != zq:
                            continue
                        for b in ((0, 0), (0, 1), (1, 0), (1, 1)):
                            if sum(b) != q:
                                continue
                            for c in ((0, 0), (0, 1), (1, 0), (1, 1)):
                                if sum(c) != r:
                                    continue
                                to = corner_index(a[0], b[0], c[0])
                                of = corner_index(a[1], b[1], c[1])
                                for i, j in ((k1, k2),) if k1 == k2 else ((k1, k2), (k2, k1)):
                                    term = s * values[of, j]
                                    key = (to, i)
                                    acc[key] = term if key not in acc else acc[key] + term
    return acc


def fold_lanes(acc, k, b):
    total = acc[corner_index(0, b, 0), k]
    for a, c in ((0, 1), (1, 0), (1, 1)):
        total = total + pltpu.roll(acc[corner_index(a, b, c), k], a * ZS + c, 1)
    return total


def krylov_kernel(last, v_own, v_low, v_up, ext, p_low, p_up, place, basis, sums, coefs):
    lane = lax.broadcasted_iota(jnp.int32, (16, 128), 1)
    layer = jnp.zeros((16, 128), jnp.int32)
    for z in range(1, 6):
        layer = layer + (lane >= z * ZS).astype(jnp.int32)
    y = lane - layer * ZS - LOW
    inside = layer < 5
    take_low = inside & (y >= -LOW) & (y <= 0)
    take_up = inside & (y >= CY) & (y <= CY + 2)

    for n in range(6):
        both = jnp.concatenate([p_low[n // 3], p_up[n // 3]], axis=1)
        coefs[n * ROWS : n * ROWS + ROWS, :] = ext[n] + dot_right(both, place[n % 3])

    def coef_main(n, zq, q, r):
        row = n * ROWS + (zq * 3 + q) * 8
        return coefs[row : row + 8, r * 128 : r * 128 + 128]

    def coef_last(n, zq, q, r):
        row = n * ROWS + 72 + zq * 3 + q
        return jnp.broadcast_to(coefs[row : row + 1, r * 128 : r * 128 + 128], (8, 128))

    v0 = []
    for k in range(3):
        t = v_own[k]
        t = t + jnp.where(take_low, pltpu.roll(v_low[k], 128 - CY, 1), 0.0)
        t = t + jnp.where(take_up, pltpu.roll(v_up[k], CY, 1), 0.0)
        v0.append(t)
    low_rows = [t[0:8] for t in v0]
    high_rows = [t[1:9] for t in v0]
    end_low = [jnp.broadcast_to(t[8:9], (8, 128)) for t in v0]
    end_high = [jnp.broadcast_to(t[9:10], (8, 128)) for t in v0]

    sub = lax.broadcasted_iota(jnp.int32, (8, 128), 0)
    y8 = y[0:8]
    owned = inside[0:8] & (sub >= LOW) & (sub < LOW + CX + last[0]) & (y8 >= 0) & (y8 < CY + last[1])

    vs = [low_rows]
    extra = product(coef_last, gather_corners(end_low, end_high))
    for it in range(3):
        acc = product(coef_main, gather_corners(low_rows, high_rows))
        new_low, new_high = [], []
        for k in range(3):
            o0 = fold_lanes(acc, k, 0)
            o1 = fold_lanes(acc, k, 1)
            new_low.append(o0 + pltpu.roll(o1, 1, 0))
            if it < 2:
                shifted = pltpu.roll(o0, 7, 0)
                if it == 0:
                    shifted = jnp.where(sub == 7, fold_lanes(extra, k, 0), shifted)
                new_high.append(shifted + o1)
        low_rows, high_rows = new_low, new_high
        vs.append(low_rows)

    for i in range(4):
        for k in range(3):
            basis[i, k] = vs[i][k]

    zero = jnp.zeros((8, 128), F32)
    high = zero
    low = zero
    for j in range(6):
        a, b = vs[j // 2], vs[(j + 1) // 2]
        total = None
        for k in range(3):
            p, e = two_prod(jnp.where(owned, a[k], 0.0), b[k])
            term = (jnp.where(owned, p, 0.0), jnp.where(owned, e, 0.0))
            total = term if total is None else df_add(total, term)
        for s in (4, 2, 1):
            total = df_add(total, (pltpu.roll(total[0], s, 0), pltpu.roll(total[1], s, 0)))
        high = jnp.where(sub == j, total[0], high)
        low = jnp.where(sub == j, total[1], low)
    total = (high, low)
    for s in (64, 32, 16, 8, 4, 2, 1):
        total = df_add(total, (pltpu.roll(total[0], s, 1), pltpu.roll(total[1], s, 1)))
    lane8 = lane[0:8]
    row = jnp.where(lane8 == sub, total[0], 0.0) + jnp.where(lane8 == sub + 8, total[1], 0.0)
    row = jnp.sum(row, axis=0, keepdims=True)
    sums[...] = jnp.broadcast_to(row, sums.shape)


def add_rows(rows):
    lane = lax.broadcasted_iota(jnp.int32, rows.shape, 1)
    lows = pltpu.roll(rows, 120, 1)
    total = (jnp.where(lane < 8, rows, 0.0), jnp.where(lane < 8, lows, 0.0))
    n = rows.shape[0]
    while n > 8:
        n //= 2
        total = df_add((total[0][:n], total[1][:n]), (total[0][n:], total[1][n:]))
    s = n // 2
    while s >= 1:
        total = df_add(total, (pltpu.roll(total[0], s, 0), pltpu.roll(total[1], s, 0)))
        s //= 2
    return total


def partial_kernel(rows, out):
    high, low = add_rows(rows[...])
    row = high + pltpu.roll(low, 8, 1)
    out[...] = jnp.broadcast_to(row[0:1], out.shape)


def finish_kernel(rows, basis, inc, res):
    high, low = add_rows(rows[...])
    high, low = high[0:1], low[0:1]
    lane = lax.broadcasted_iota(jnp.int32, (1, 128), 1)

    def splat(part, j):
        return jnp.sum(jnp.where(lane == j, part, 0.0), axis=1, keepdims=True) + jnp.zeros((8, 128), F32)

    m = [(splat(high, j), splat(low, j)) for j in range(6)]
    m = [None] + [df_div(x, m[0]) for x in m[1:]]
    mu = m[1]
    lag = {j: df_sub(m[j], df_mul(mu, m[j - 1])) for j in range(2, 6)}
    n2 = lag[2]
    lag = {j: df_sub(lag[j], df_mul(mu, lag[j - 1])) for j in range(3, 6)}
    n3 = df_sub(lag[3], df_mul(mu, n2))
    lag = {j: df_sub(lag[j], df_mul(mu, lag[j - 1])) for j in range(4, 6)}
    n4 = df_sub(lag[4], df_mul(mu, n3))
    n5 = df_sub(df_sub(lag[5], df_mul(mu, lag[4])), df_mul(mu, n4))
    a1 = df_div(n3, n2)
    h2 = df_sub(df_sub(n4, df_mul(a1, n3)), df_mul(n2, n2))
    b2 = df_div(h2, n2)
    t = df_sub(df_sub(n5, df_mul(a1, n4)), df_mul(n2, n3))
    a2 = df_sub(df_div(t, h2), a1)
    two = (jnp.full((8, 128), RIDGE, F32), jnp.zeros((8, 128), F32))
    y0 = df_neg(df_add(two, mu))
    p2 = df_sub(df_mul(df_sub(y0, a1), y0), n2)
    p3 = df_sub(df_mul(df_sub(y0, a2), p2), df_mul(b2, y0))
    c2 = df_neg(df_add(a1, a2))
    c1 = df_sub(df_sub(df_mul(a1, a2), n2), b2)
    c0 = df_mul(a2, n2)
    q1 = df_add(y0, c2)
    q0 = df_add(df_mul(y0, q1), c1)
    s = 1.0 / p3[0]
    r3, r2, r1, r0 = s, s * c2[0], s * c1[0], s * c0[0]
    u2, u1, u0 = -s, -s * q1[0], -s * q0[0]
    mu = mu[0]
    for k in range(3):
        v = [basis[i, k] for i in range(4)]
        w1 = v[1] - mu * v[0]
        w2a = v[2] - mu * v[1]
        w2 = w2a - mu * w1
        w3 = v[3] - mu * v[2]
        w3 = w3 - mu * w2a
        w3 = w3 - mu * w2
        r = r3 * w3 + r2 * w2 + r1 * w1 + r0 * v[0]
        u = u2 * w2 + u1 * w1 + u0 * v[0]
        for z in range(CZ + 1):
            first = z * ZS + LOW
            inc[k, z] = u[LOW : LOW + CX, first : first + CY]
            res[k, z] = r[LOW : LOW + CX, first : first + CY]


VM = pl.BlockSpec(memory_space=pltpu.VMEM)
SM = pl.BlockSpec(memory_space=pltpu.SMEM)


def call(kernel, outs, ins, scratch=(), name=None):
    shapes = [jax.ShapeDtypeStruct(s, F32) for s in outs]
    specs = [SM if jnp.ndim(x) == 1 else VM for x in ins]
    return pl.pallas_call(
        kernel,
        out_shape=shapes,
        in_specs=specs,
        out_specs=[VM] * len(shapes),
        scratch_shapes=list(scratch),
        name=name,
        compiler_params=pltpu.CompilerParams(vmem_limit_bytes=48 * 2**20),
    )(*ins)


def upward(x, axis):
    n = lax.axis_size(axis)
    return lax.ppermute(x, axis, [(i, i + 1) for i in range(n - 1)])


def downward(x, axis):
    n = lax.axis_size(axis)
    return lax.ppermute(x, axis, [(i + 1, i) for i in range(n - 1)])


def body(reference_image, moving_image, image_gradient, voxel_shift, subvoxel):
    gz = moving_image.shape[0]
    shift = voxel_shift.reshape(-1)
    frac = subvoxel.reshape(-1)
    last = jnp.stack(
        [
            (lax.axis_index(GX) == lax.axis_size(GX) - 1).astype(jnp.int32),
            (lax.axis_index(GY) == lax.axis_size(GY) - 1).astype(jnp.int32),
        ]
    )

    mx_low = upward(moving_image[:, 24:32, :], GX)
    mx_up = downward(moving_image[:, 0:8, :], GX)

    own, s_up, s_low = call(
        stiff_kernel,
        [(6, ROWS, 384), (6, 32, 384), (6, 32, 384)],
        [image_gradient, bf(stiff_y_weights()), bf(stiff_x_weights())],
        [pltpu.VMEM((6 * 96, CZ * 128), F32)],
        name="stiff",
    )
    sx_low = upward(s_up, GX)
    sx_up = downward(s_low, GX)

    strip_up, strip_low = call(strip_kernel, [(3, 48, 128)] * 2, [moving_image, mx_low, mx_up], name="strip")
    my_low = upward(strip_up, GY)
    my_up = downward(strip_low, GY)

    plo, phi = place_x()
    ext, p_up, p_low = call(
        extend_kernel,
        [(6, ROWS, 384), (2, ROWS, 128), (2, ROWS, 128)],
        [own, sx_low, sx_up, bf(plo), bf(phi), bf(pack_y())],
        name="extend",
    )
    py_low = upward(p_up, GY)
    py_up = downward(p_low, GY)

    (load,) = call(
        warp_kernel,
        [(3, 8, 128)],
        [shift, frac, moving_image, mx_low, mx_up, my_low, my_up, reference_image, image_gradient,
         bf(load_y_weights()), bf(load_x_weights())],
        [pltpu.VMEM((2, gz, 48, 128), F32), pltpu.VMEM((96, 2 * CZ * 128), F32)],
        name="warp",
    )
    lx_low = upward(load, GX)
    lx_up = downward(load, GX)
    pad = lambda x, a, b: jnp.pad(x, ((0, 0), (a, b), (0, 0)))
    v_own = pad(load, 0, 8) + pad(lx_low[:, 4:8], 0, 12) + pad(lx_up[:, 3:6], 7, 6)
    v_low = upward(v_own, GY)
    v_up = downward(v_own, GY)

    nx, ny = lax.axis_size(GX), lax.axis_size(GY)
    basis, sums = call(
        krylov_kernel,
        [(4, 3, 8, 128), (nx, 128)],
        [last, v_own, v_low, v_up, ext, py_low, py_up, bf(place_y())],
        [pltpu.VMEM((6 * ROWS, 384), F32)],
        name="krylov",
    )
    rows = lax.all_to_all(sums, GX, 0, 0, tiled=True)
    (sums,) = call(partial_kernel, [(ny, 128)], [rows], name="partial")
    rows = lax.all_to_all(sums, GY, 0, 0, tiled=True)
    inc, res = call(finish_kernel, [(3, CZ + 1, CX, CY)] * 2, [rows, basis], name="finish")
    return inc, res


def solution(mesh, shape=(4, 2, 4, 8)):
    torus = Mesh(mesh.devices.reshape(shape), GX + GY)
    placed = (
        P(None, GX, GY),
        P(None, GX, GY),
        P(None, None, GX, GY),
        P(None, None, GX, GY),
        P(None, None, GX, GY),
    )
    return jax.shard_map(
        body,
        mesh=torus,
        in_specs=placed,
        out_specs=(P(None, None, GX, GY), P(None, None, GX, GY)),
        check_vma=False,
    )
```

time: 1580 us -> 100 us (0.06); the launches traced: 1550 us -> 99 us
  local copies, waits for them, and re-layouts: 1230 us -> 4.34 us
  blocking collectives: 197 us -> 27.6 us
  other arithmetic: 27.2 us -> 0.09 us
  starting transfers between devices: 60.2 us -> 40.2 us
  Pallas kernels: 0 us -> 19.6 us
    gather x1070 -> x0, local copies, waits for them, and re-layouts: 1120 us -> none
    psum x20 -> x0, blocking collectives: 197 us -> none  [one_axis_at_a_time(): return functools.reduce(lax.psum, axes, x)]
    convert_element_type x16 -> x0, local copies, waits for them, and re-layouts: 83.7 us -> none  [the longest x12 64.3 us: body(): element_major(image_gradient[component], count_z, count_x, count_y)]
    all_to_all x0 -> x2, blocking collectives: none -> 27.6 us  [the longest x1 17.5 us: body(): rows = lax.all_to_all(sums, GY, 0, 0, tiled=True)]
    ppermute x20 -> x12, starting transfers between devices: 60.2 us -> 40.2 us  [the longest x6 22.5 us: downward(): return lax.ppermute(x, axis, [(i + 1, i) for i in range(n - 1)])]
    pallas_call x0 -> x7, Pallas kernels: none -> 19.6 us  [call(): pl.pallas_call(kernel, out_shape=shapes, in_specs=specs, out_specs=[VM] *...]
  transfers between devices with their start and end apart: 20 -> 12, of which waited for: 11 -> 5; matrix products, arithmetic and copies ran while one was open for 38% -> 0% of each run, Pallas kernels for 0% -> 16%
where the time goes in v1:
time: 100 us; the launch traced here: 99 us
  starting transfers between devices  40.2 us (40%)
  blocking collectives  27.6 us (28%)
  Pallas kernels  19.6 us (20%)
  waiting for transfers between devices  6.28 us (6%)
  local copies, waits for them, and re-layouts  4.34 us (4%)
    ppermute x6, starting transfers between devices, downward(): return lax.ppermute(x, axis, [(i + 1, i) for i in range(n - 1)])  22.5 us
    pallas_call x7, Pallas kernels, call(): pl.pallas_call(kernel, out_shape=shapes, in_specs=specs, out_specs=[VM] *...  19.6 us
    ppermute x6, starting transfers between devices, upward(): return lax.ppermute(x, axis, [(i, i + 1) for i in range(n - 1)])  17.7 us
    all_to_all x1, blocking collectives, body(): rows = lax.all_to_all(sums, GY, 0, 0, tiled=True)  17.5 us
    all_to_all x1, blocking collectives, body(): rows = lax.all_to_all(sums, GX, 0, 0, tiled=True)  10.1 us
    ppermute x6, waiting for transfers between devices, downward(): return lax.ppermute(x, axis, [(i + 1, i) for i in range(n - 1)])  3.2 us
    ppermute x6, waiting for transfers between devices, upward(): return lax.ppermute(x, axis, [(i, i + 1) for i in range(n - 1)])  3.09 us
    unnamed x28, local copies, waits for them, and re-layouts  3.08 us
  transfers between devices with their start and end apart: 12, of which 5 were waited for; matrix products, arithmetic and copies ran while one was open for 0% of the time, Pallas kernels for 16%

profile of v1, /device:TPU:8, one launch (start us, length us, event | category | flops | bytes accessed | tf_op | source)
XLA Modules:
  0.0 99.0 jit_solution(10099389990451405067)
XLA Ops:
  0.6 0.0 copy-start.5
  0.6 0.0 copy-start.8
  0.7 1.1 %fusion = (f32[44,8,128]{2,1,0:T(8,128)S(1)}, f32[44,8,128]{2,1,0:T(8,128)S(1)}) fusion(f32[44,32,128]{2,1,0:T(8,128)} %mov.3), kind=kLoop, calls=%fused_computation.2 | loop fusion | bytes 720896 | tf_op jit(solution)/shard_map/slice | solution.py:569
  1.7 0.0 copy-start
  1.8 1.4 %collective-permute-start.1 = (f32[44,8,128]{2,1,0:T(8,128)S(1)}, f32[44,8,128]{2,1,0:T(8,128)S(1)}, u32[]{:S(2)}, u32[]{:S(2)}) collective-permute-start(f32[44,8,128]{2,1,0:T(8,128)S(1)} %get-tuple-element.22), channel_id=1, source_target_pairs={{32,0},{64,32},{96,64},{128,96},{160,128},{192,160},{224,192},{33,... | collective-permute-start | bytes 540680 | tf_op jit(solution)/shard_map/ppermute | solution.py:554
  3.2 3.0 %collective-permute-start = (f32[44,8,128]{2,1,0:T(8,128)S(1)}, f32[44,8,128]{2,1,0:T(8,128)S(1)}, u32[]{:S(2)}, u32[]{:S(2)}) collective-permute-start(f32[44,8,128]{2,1,0:T(8,128)S(1)} %get-tuple-element.23), channel_id=1, source_target_pairs={{0,32},{32,64},{64,96},{96,128},{128,160},{160,192},{192,224},{1,3... | collective-permute-start | bytes 540680 | tf_op jit(solution)/shard_map/ppermute | solution.py:549
  6.2 0.0 copy-done.5
  6.2 0.0 copy-done.8
  6.3 0.0 copy-start.1
  6.3 1.1 %copy-done.1 = bf16[3,32,32,128]{3,2,1,0:T(8,128)(2,1)S(1)} copy-done((bf16[3,32,32,128]{3,2,1,0:T(8,128)(2,1)S(1)}, bf16[3,32,32,128]{3,2,1,0:T(8,128)(2,1)}, u32[]{:S(2)}) %copy-start.1) | copy-done | bytes 786456
  7.4 4.3 %stiff.1 = (f32[6,96,384]{2,1,0:T(8,128)S(1)}, f32[6,32,384]{2,1,0:T(8,128)}, f32[6,32,384]{2,1,0:T(8,128)}) custom-call(bf16[3,32,32,128]{3,2,1,0:T(8,128)(2,1)S(1)} %copy-done.1, bf16[512,384]{1,0:T(8,128)(2,1)S(1)} %copy-done.5, bf16[160,96]{1,0:T(8,128)(2,1)S(1)} %copy-done.8), custom_call_target="tpu_custom_call" | custom-call | tf_op jit(solution)/shard_map/stiff/pallas_call | solution.py:536
  11.7 0.0 copy-start.2
  11.7 3.8 %collective-permute-start.8 = (f32[6,32,384]{2,1,0:T(8,128)}, f32[6,32,384]{2,1,0:T(8,128)}, u32[]{:S(2)}, u32[]{:S(2)}) collective-permute-start(f32[6,32,384]{2,1,0:T(8,128)} %get-tuple-element.15), channel_id=1, source_target_pairs={{0,32},{32,64},{64,96},{96,128},{128,160},{160,192},{192,224},{1,3... | collective-permute-start | bytes 884744 | tf_op jit(solution)/shard_map/ppermute | solution.py:549
  15.6 0.0 copy-start.12
  15.6 1.4 %collective-permute-start.9 = (f32[6,32,384]{2,1,0:T(8,128)}, f32[6,32,384]{2,1,0:T(8,128)}, u32[]{:S(2)}, u32[]{:S(2)}) collective-permute-start(f32[6,32,384]{2,1,0:T(8,128)} %get-tuple-element.16), channel_id=1, source_target_pairs={{32,0},{64,32},{96,64},{128,96},{160,128},{192,160},{224,192},{33,... | collective-permute-start | bytes 884744 | tf_op jit(solution)/shard_map/ppermute | solution.py:554
  17.0 0.0 collective-permute-done.1.from_up.x_up
  17.0 0.0 collective-permute-done.from_low.x_low
  17.0 0.0 copy-done
  17.0 1.2 %strip.1 = (f32[3,48,128]{2,1,0:T(8,128)}, f32[3,48,128]{2,1,0:T(8,128)}) custom-call(f32[44,32,128]{2,1,0:T(8,128)S(1)} %copy-done, f32[44,8,128]{2,1,0:T(8,128)S(1)} %collective-permute-done.from_low.x_low, f32[44,8,128]{2,1,0:T(8,128)S(1)} %collective-permute-done.1.from_up.x_up), custom_call_target="tpu_custom_call" | custom-call | tf_op jit(solution)/shard_map/strip/pallas_call | solution.py:536
  18.3 0.0 copy-start.13
  18.3 4.0 %collective-permute-start.2 = (f32[3,48,128]{2,1,0:T(8,128)}, f32[3,48,128]{2,1,0:T(8,128)S(1)}, u32[]{:S(2)}, u32[]{:S(2)}) collective-permute-start(f32[3,48,128]{2,1,0:T(8,128)} %get-tuple-element.12), channel_id=1, source_target_pairs={{0,1},{1,2},{2,3},{3,4},{4,5},{5,6},{6,7},{7,8},{8,9},{9,10},{10,1... | collective-permute-start | bytes 221192 | tf_op jit(solution)/shard_map/ppermute | solution.py:549
  22.2 5.7 %collective-permute-start.3 = (f32[3,48,128]{2,1,0:T(8,128)}, f32[3,48,128]{2,1,0:T(8,128)S(1)}, u32[]{:S(2)}, u32[]{:S(2)}) collective-permute-start(f32[3,48,128]{2,1,0:T(8,128)} %get-tuple-element.13), channel_id=1, source_target_pairs={{1,0},{2,1},{3,2},{4,3},{5,4},{6,5},{7,6},{8,7},{9,8},{10,9},{11,1... | collective-permute-start | bytes 221192 | tf_op jit(solution)/shard_map/ppermute | solution.py:554
  28.0 0.0 copy-done.12
  28.0 0.1 reshape.14.shift
  28.1 0.0 copy-done.13
  28.1 0.0 copy-start.11
  28.1 0.1 reshape.15.frac
  28.2 0.0 copy-start.4
  28.2 0.8 collective-permute-done.2.y_low
  28.9 1.8 %collective-permute-done.3.y_up = f32[3,48,128]{2,1,0:T(8,128)S(1)} collective-permute-done((f32[3,48,128]{2,1,0:T(8,128)}, f32[3,48,128]{2,1,0:T(8,128)S(1)}, u32[]{:S(2)}, u32[]{:S(2)}) %collective-permute-start.3) | collective-permute-done | bytes 73760 | tf_op jit(solution)/shard_map/ppermute | solution.py:554
  30.8 0.0 copy-done.2
  30.8 0.0 copy-done.11
  30.8 0.9 copy-done.6
  31.7 0.0 copy-start.7
  31.7 0.9 copy-done.7
  32.7 7.4 %warp.1 = f32[3,8,128]{2,1,0:T(8,128)S(1)} custom-call(s32[768]{0:T(1024)S(1)} %reshape.14.shift, f32[768]{0:T(1024)S(1)} %reshape.15.frac, f32[44,32,128]{2,1,0:T(8,128)S(1)} %copy-done, f32[44,8,128]{2,1,0:T(8,128)S(1)} %collective-permute-done.from_low.x_low, f32[44,8,128]{2,1,0:T(8,128)S(1)} %collective-permute-done.1.from_up.x_up, ...), custom_call_target="tpu_custom_call" | custom-call | tf_op jit(solution)/shard_map/warp/pallas_call | solution.py:536
  40.1 1.3 %collective-permute-start.5 = (f32[3,8,128]{2,1,0:T(8,128)S(1)}, f32[3,8,128]{2,1,0:T(8,128)S(1)}, u32[]{:S(2)}, u32[]{:S(2)}) collective-permute-start(f32[3,8,128]{2,1,0:T(8,128)S(1)} %warp.1), channel_id=1, source_target_pairs={{32,0},{64,32},{96,64},{128,96},{160,128},{192,160},{224,192},{33,... | collective-permute-start | bytes 36872 | tf_op jit(solution)/shard_map/ppermute | solution.py:554
  41.5 3.0 %collective-permute-start.4 = (f32[3,8,128]{2,1,0:T(8,128)S(1)}, f32[3,8,128]{2,1,0:T(8,128)S(1)}, u32[]{:S(2)}, u32[]{:S(2)}) collective-permute-start(f32[3,8,128]{2,1,0:T(8,128)S(1)} %warp.1), channel_id=1, source_target_pairs={{0,32},{32,64},{64,96},{96,128},{128,160},{160,192},{192,224},{1,3... | collective-permute-start | bytes 36872 | tf_op jit(solution)/shard_map/ppermute | solution.py:549
  44.5 0.0 collective-permute-done.5
  44.5 0.8 collective-permute-done.4
  45.3 0.0 copy-start.9
  45.3 0.0 copy-start.10
  45.3 6.5 %collective-permute-start.7 = (f32[3,16,128]{2,1,0:T(8,128)S(1)}, f32[3,16,128]{2,1,0:T(8,128)S(1)}, u32[]{:S(2)}, u32[]{:S(2)}) collective-permute-start(f32[3,16,128]{2,1,0:T(8,128)S(1)} %pad_add_fusion.v_own), channel_id=1, source_target_pairs={{1,0},{2,1},{3,2},{4,3},{5,4},{6,5},{7,6},{8,7},{9,8},{10,9},{11,1... | collective-permute-start | bytes 73736 | tf_op jit(solution)/shard_map/ppermute | solution.py:554
  51.9 1.9 %collective-permute-start.6 = (f32[3,16,128]{2,1,0:T(8,128)S(1)}, f32[3,16,128]{2,1,0:T(8,128)S(1)}, u32[]{:S(2)}, u32[]{:S(2)}) collective-permute-start(f32[3,16,128]{2,1,0:T(8,128)S(1)} %pad_add_fusion.v_own), channel_id=1, source_target_pairs={{0,1},{1,2},{2,3},{3,4},{4,5},{5,6},{6,7},{7,8},{8,9},{9,10},{10,1... | collective-permute-start | bytes 73736 | tf_op jit(solution)/shard_map/ppermute | solution.py:549
  53.8 0.0 collective-permute-done.8.from_low
  53.8 0.0 collective-permute-done.9.from_up
  53.8 0.0 copy-done.4
  53.8 0.0 copy-done.9
  53.9 0.0 copy-done.10
  53.9 0.0 copy-start.3
  53.9 2.8 %extend.1 = (f32[6,96,384]{2,1,0:T(8,128)S(1)}, f32[2,96,128]{2,1,0:T(8,128)S(1)}, f32[2,96,128]{2,1,0:T(8,128)S(1)}) custom-call(f32[6,96,384]{2,1,0:T(8,128)S(1)} %get-tuple-element.14.own, f32[6,32,384]{2,1,0:T(8,128)} %collective-permute-done.8.from_low, f32[6,32,384]{2,1,0:T(8,128)} %collective-permute-done.9.from_up, bf16[96,32]{1,0:T(8,128)(2,1)S(1)} %copy-done.10, ...), custom_call_target="tpu_custom_call" | custom-call | tf_op jit(solution)/shard_map/extend/pallas_call | solution.py:536
  56.7 1.9 %collective-permute-start.10 = (f32[2,96,128]{2,1,0:T(8,128)S(1)}, f32[2,96,128]{2,1,0:T(8,128)S(1)}, u32[]{:S(2)}, u32[]{:S(2)}) collective-permute-start(f32[2,96,128]{2,1,0:T(8,128)S(1)} %get-tuple-element.18), channel_id=1, source_target_pairs={{0,1},{1,2},{2,3},{3,4},{4,5},{5,6},{6,7},{7,8},{8,9},{9,10},{10,1... | collective-permute-start | bytes 294920 | tf_op jit(solution)/shard_map/ppermute | solution.py:549
  58.7 6.0 %collective-permute-start.11 = (f32[2,96,128]{2,1,0:T(8,128)S(1)}, f32[2,96,128]{2,1,0:T(8,128)S(1)}, u32[]{:S(2)}, u32[]{:S(2)}) collective-permute-start(f32[2,96,128]{2,1,0:T(8,128)S(1)} %get-tuple-element.19), channel_id=1, source_target_pairs={{1,0},{2,1},{3,2},{4,3},{5,4},{6,5},{7,6},{8,7},{9,8},{10,9},{11,1... | collective-permute-start | bytes 294920 | tf_op jit(solution)/shard_map/ppermute | solution.py:554
  64.7 0.1 add_convert_fusion.last
  64.8 0.0 collective-permute-done.7.v_up
  64.8 0.0 collective-permute-done.6.v_low
  64.8 1.5 %collective-permute-done.10.p_low = f32[2,96,128]{2,1,0:T(8,128)S(1)} collective-permute-done((f32[2,96,128]{2,1,0:T(8,128)S(1)}, f32[2,96,128]{2,1,0:T(8,128)S(1)}, u32[]{:S(2)}, u32[]{:S(2)}) %collective-permute-start.10) | collective-permute-done | bytes 98336 | tf_op jit(solution)/shard_map/ppermute | solution.py:549
  66.3 1.3 %collective-permute-done.11.p_up = f32[2,96,128]{2,1,0:T(8,128)S(1)} collective-permute-done((f32[2,96,128]{2,1,0:T(8,128)S(1)}, f32[2,96,128]{2,1,0:T(8,128)S(1)}, u32[]{:S(2)}, u32[]{:S(2)}) %collective-permute-start.11) | collective-permute-done | bytes 98336 | tf_op jit(solution)/shard_map/ppermute | solution.py:554
  67.7 0.0 copy-done.3
  67.7 2.4 %krylov.1 = (f32[4,3,8,128]{3,2,1,0:T(8,128)S(1)}, f32[8,128]{1,0:T(8,128)S(1)}) custom-call(s32[2]{0:T(128)S(1)} %add_convert_fusion.last, f32[3,16,128]{2,1,0:T(8,128)S(1)} %pad_add_fusion.v_own, f32[3,16,128]{2,1,0:T(8,128)S(1)} %collective-permute-done.6.v_low, f32[3,16,128]{2,1,0:T(8,128)S(1)} %collective-permute-done.7.v_up, ...), custom_call_target="tpu_custom_call" | custom-call | tf_op jit(solution)/shard_map/krylov/pallas_call | solution.py:536
  70.1 10.1 %all_to_all.22 = f32[8,1,128]{2,1,0:T(1,128)S(1)} all-to-all(f32[8,1,128]{2,1,0:T(1,128)S(1)} %bitcast.13), channel_id=1, replica_groups=mesh['gx_0'=4,'gx_1'=2,'gy_0'=4,'gy_1'=8] {'gx_0','gx_1'}, dimensions={0} | all-to-all | bytes 8192 | tf_op jit(solution)/shard_map/all_to_all | solution.py:618
  80.1 0.2 partial.1
  80.3 17.5 %all_to_all.23 = f32[32,1,128]{2,1,0:T(1,128)S(1)} all-to-all(f32[32,1,128]{2,1,0:T(1,128)S(1)} %bitcast.10), channel_id=1, replica_groups=mesh['gx_0'=4,'gx_1'=2,'gy_0'=4,'gy_1'=8] {'gy_0','gy_1'}, dimensions={0} | all-to-all | bytes 32768 | tf_op jit(solution)/shard_map/all_to_all | solution.py:620
  97.9 1.2 %finish.1 = (f32[3,5,4,16]{3,2,1,0:T(4,128)}, f32[3,5,4,16]{3,2,1,0:T(4,128)}) custom-call(f32[32,128]{1,0:T(8,128)S(1)} %bitcast.11, f32[4,3,8,128]{3,2,1,0:T(8,128)S(1)} %get-tuple-element.21.basis), custom_call_target="tpu_custom_call" | custom-call | tf_op jit(solution)/shard_map/finish/pallas_call | solution.py:536
  (4 shorter events, 0.0 us)
Async XLA Ops:
  0.6 5.6 %copy-start.5 = (bf16[512,384]{1,0:T(8,128)(2,1)S(1)}, bf16[512,384]{1,0:T(8,128)(2,1)}, u32[]{:S(2)}) copy-start(bf16[512,384]{1,0:T(8,128)(2,1)} %constant.45.clone.wy) | copy-start | bytes 1179652
  0.6 5.6 %copy-start.8 = (bf16[160,96]{1,0:T(8,128)(2,1)S(1)}, bf16[160,96]{1,0:T(8,128)(2,1)}, u32[]{:S(2)}) copy-start(bf16[160,96]{1,0:T(8,128)(2,1)} %constant.46.clone.wx) | copy-start | bytes 92164
  1.7 15.3 %copy-start = (f32[44,32,128]{2,1,0:T(8,128)S(1)}, f32[44,32,128]{2,1,0:T(8,128)}, u32[]{:S(2)}) copy-start(f32[44,32,128]{2,1,0:T(8,128)} %mov.3) | copy-start | bytes 2162692
  1.8 15.2 %collective-permute-start.1 = (f32[44,8,128]{2,1,0:T(8,128)S(1)}, f32[44,8,128]{2,1,0:T(8,128)S(1)}, u32[]{:S(2)}, u32[]{:S(2)}) collective-permute-start(f32[44,8,128]{2,1,0:T(8,128)S(1)} %get-tuple-element.22), channel_id=1, source_target_pairs={{32,0},{64,32},{96,64},{128,96},{160,128},{192,160},{224,192},{33,... | collective-permute-start | bytes 540680 | tf_op jit(solution)/shard_map/ppermute | solution.py:554
  3.2 13.8 %collective-permute-start = (f32[44,8,128]{2,1,0:T(8,128)S(1)}, f32[44,8,128]{2,1,0:T(8,128)S(1)}, u32[]{:S(2)}, u32[]{:S(2)}) collective-permute-start(f32[44,8,128]{2,1,0:T(8,128)S(1)} %get-tuple-element.23), channel_id=1, source_target_pairs={{0,32},{32,64},{64,96},{96,128},{128,160},{160,192},{192,224},{1,3... | collective-permute-start | bytes 540680 | tf_op jit(solution)/shard_map/ppermute | solution.py:549
  6.3 1.1 %copy-start.1 = (bf16[3,32,32,128]{3,2,1,0:T(8,128)(2,1)S(1)}, bf16[3,32,32,128]{3,2,1,0:T(8,128)(2,1)}, u32[]{:S(2)}) copy-start(bf16[3,32,32,128]{3,2,1,0:T(8,128)(2,1)} %grad.3) | copy-start | bytes 2359300
  11.7 19.1 %copy-start.2 = (bf16[3,32,32,128]{3,2,1,0:T(8,128)(2,1)S(1)}, bf16[3,32,32,128]{3,2,1,0:T(8,128)(2,1)}, u32[]{:S(2)}) copy-start(bf16[3,32,32,128]{3,2,1,0:T(8,128)(2,1)} %grad.3) | copy-start | bytes 2359300
  11.7 42.1 %collective-permute-start.8 = (f32[6,32,384]{2,1,0:T(8,128)}, f32[6,32,384]{2,1,0:T(8,128)}, u32[]{:S(2)}, u32[]{:S(2)}) collective-permute-start(f32[6,32,384]{2,1,0:T(8,128)} %get-tuple-element.15), channel_id=1, source_target_pairs={{0,32},{32,64},{64,96},{96,128},{128,160},{160,192},{192,224},{1,3... | collective-permute-start | bytes 884744 | tf_op jit(solution)/shard_map/ppermute | solution.py:549
  15.6 12.4 %copy-start.12 = (s32[3,4,4,16]{3,2,1,0:T(4,128)S(1)}, s32[3,4,4,16]{3,2,1,0:T(4,128)}, u32[]{:S(2)}) copy-start(s32[3,4,4,16]{3,2,1,0:T(4,128)} %param.16) | copy-start | bytes 9220
  15.6 38.3 %collective-permute-start.9 = (f32[6,32,384]{2,1,0:T(8,128)}, f32[6,32,384]{2,1,0:T(8,128)}, u32[]{:S(2)}, u32[]{:S(2)}) collective-permute-start(f32[6,32,384]{2,1,0:T(8,128)} %get-tuple-element.16), channel_id=1, source_target_pairs={{32,0},{64,32},{96,64},{128,96},{160,128},{192,160},{224,192},{33,... | collective-permute-start | bytes 884744 | tf_op jit(solution)/shard_map/ppermute | solution.py:554
  18.3 9.8 %copy-start.13 = (f32[3,4,4,16]{3,2,1,0:T(4,128)S(1)}, f32[3,4,4,16]{3,2,1,0:T(4,128)}, u32[]{:S(2)}) copy-start(f32[3,4,4,16]{3,2,1,0:T(4,128)} %param.17) | copy-start | bytes 9220
  18.3 10.7 %collective-permute-start.2 = (f32[3,48,128]{2,1,0:T(8,128)}, f32[3,48,128]{2,1,0:T(8,128)S(1)}, u32[]{:S(2)}, u32[]{:S(2)}) collective-permute-start(f32[3,48,128]{2,1,0:T(8,128)} %get-tuple-element.12), channel_id=1, source_target_pairs={{0,1},{1,2},{2,3},{3,4},{4,5},{5,6},{6,7},{7,8},{8,9},{9,10},{10,1... | collective-permute-start | bytes 221192 | tf_op jit(solution)/shard_map/ppermute | solution.py:549
  22.2 8.5 %collective-permute-start.3 = (f32[3,48,128]{2,1,0:T(8,128)}, f32[3,48,128]{2,1,0:T(8,128)S(1)}, u32[]{:S(2)}, u32[]{:S(2)}) collective-permute-start(f32[3,48,128]{2,1,0:T(8,128)} %get-tuple-element.13), channel_id=1, source_target_pairs={{1,0},{2,1},{3,2},{4,3},{5,4},{6,5},{7,6},{8,7},{9,8},{10,9},{11,1... | collective-permute-start | bytes 221192 | tf_op jit(solution)/shard_map/ppermute | solution.py:554
  28.1 2.7 %copy-start.11 = (bf16[8,32]{1,0:T(8,128)(2,1)S(1)}, bf16[8,32]{1,0:T(8,128)(2,1)}, u32[]{:S(2)}) copy-start(bf16[8,32]{1,0:T(8,128)(2,1)} %constant.51.clone.wlx) | copy-start | bytes 1540
  28.2 25.7 %copy-start.4 = (bf16[1152,256]{1,0:T(8,128)(2,1)S(1)}, bf16[1152,256]{1,0:T(8,128)(2,1)}, u32[]{:S(2)}) copy-start(bf16[1152,256]{1,0:T(8,128)(2,1)} %constant.49.clone.pack) | copy-start | bytes 1769476
  30.8 1.0 copy-start.6
  31.7 0.9 copy-start.7
  40.1 4.4 %collective-permute-start.5 = (f32[3,8,128]{2,1,0:T(8,128)S(1)}, f32[3,8,128]{2,1,0:T(8,128)S(1)}, u32[]{:S(2)}, u32[]{:S(2)}) collective-permute-start(f32[3,8,128]{2,1,0:T(8,128)S(1)} %warp.1), channel_id=1, source_target_pairs={{32,0},{64,32},{96,64},{128,96},{160,128},{192,160},{224,192},{33,... | collective-permute-start | bytes 36872 | tf_op jit(solution)/shard_map/ppermute | solution.py:554
  41.5 3.9 %collective-permute-start.4 = (f32[3,8,128]{2,1,0:T(8,128)S(1)}, f32[3,8,128]{2,1,0:T(8,128)S(1)}, u32[]{:S(2)}, u32[]{:S(2)}) collective-permute-start(f32[3,8,128]{2,1,0:T(8,128)S(1)} %warp.1), channel_id=1, source_target_pairs={{0,32},{32,64},{64,96},{96,128},{128,160},{160,192},{192,224},{1,3... | collective-permute-start | bytes 36872 | tf_op jit(solution)/shard_map/ppermute | solution.py:549
  45.3 8.5 %copy-start.9 = (bf16[96,32]{1,0:T(8,128)(2,1)S(1)}, bf16[96,32]{1,0:T(8,128)(2,1)}, u32[]{:S(2)}) copy-start(bf16[96,32]{1,0:T(8,128)(2,1)} %constant.48.clone.phi) | copy-start | bytes 18436
  45.3 8.5 %copy-start.10 = (bf16[96,32]{1,0:T(8,128)(2,1)S(1)}, bf16[96,32]{1,0:T(8,128)(2,1)}, u32[]{:S(2)}) copy-start(bf16[96,32]{1,0:T(8,128)(2,1)} %constant.47.clone.plo) | copy-start | bytes 18436
  45.3 19.4 %collective-permute-start.7 = (f32[3,16,128]{2,1,0:T(8,128)S(1)}, f32[3,16,128]{2,1,0:T(8,128)S(1)}, u32[]{:S(2)}, u32[]{:S(2)}) collective-permute-start(f32[3,16,128]{2,1,0:T(8,128)S(1)} %pad_add_fusion.v_own), channel_id=1, source_target_pairs={{1,0},{2,1},{3,2},{4,3},{5,4},{6,5},{7,6},{8,7},{9,8},{10,9},{11,1... | collective-permute-start | bytes 73736 | tf_op jit(solution)/shard_map/ppermute | solution.py:554
  51.9 12.9 %collective-permute-start.6 = (f32[3,16,128]{2,1,0:T(8,128)S(1)}, f32[3,16,128]{2,1,0:T(8,128)S(1)}, u32[]{:S(2)}, u32[]{:S(2)}) collective-permute-start(f32[3,16,128]{2,1,0:T(8,128)S(1)} %pad_add_fusion.v_own), channel_id=1, source_target_pairs={{0,1},{1,2},{2,3},{3,4},{4,5},{5,6},{6,7},{7,8},{8,9},{9,10},{10,1... | collective-permute-start | bytes 73736 | tf_op jit(solution)/shard_map/ppermute | solution.py:549
  53.9 13.8 %copy-start.3 = (bf16[3,256,384]{2,1,0:T(8,128)(2,1)S(1)}, bf16[3,256,384]{2,1,0:T(8,128)(2,1)}, u32[]{:S(2)}) copy-start(bf16[3,256,384]{2,1,0:T(8,128)(2,1)} %constant.52.clone.place) | copy-start | bytes 1769476
  56.7 9.6 %collective-permute-start.10 = (f32[2,96,128]{2,1,0:T(8,128)S(1)}, f32[2,96,128]{2,1,0:T(8,128)S(1)}, u32[]{:S(2)}, u32[]{:S(2)}) collective-permute-start(f32[2,96,128]{2,1,0:T(8,128)S(1)} %get-tuple-element.18), channel_id=1, source_target_pairs={{0,1},{1,2},{2,3},{3,4},{4,5},{5,6},{6,7},{7,8},{8,9},{9,10},{10,1... | collective-permute-start | bytes 294920 | tf_op jit(solution)/shard_map/ppermute | solution.py:549
  58.7 9.0 %collective-permute-start.11 = (f32[2,96,128]{2,1,0:T(8,128)S(1)}, f32[2,96,128]{2,1,0:T(8,128)S(1)}, u32[]{:S(2)}, u32[]{:S(2)}) collective-permute-start(f32[2,96,128]{2,1,0:T(8,128)S(1)} %get-tuple-element.19), channel_id=1, source_target_pairs={{1,0},{2,1},{3,2},{4,3},{5,4},{6,5},{7,6},{8,7},{9,8},{10,9},{11,1... | collective-permute-start | bytes 294920 | tf_op jit(solution)/shard_map/ppermute | solution.py:554
